TPU v7x, 32 devices: a whole 2x2x4 slice. The times are simulated.
32 devices in a mesh: groups: 1, ex: 16 (over z, y, core), layer: 2 (over x), pb: 1.
Axes of the slice: x: 2, y: 2, z: 4, core: 2. Of those that a mesh axis runs over, the one named last changes fastest.
Arguments:
- train_grads: float32 [2, 1536, 1024], P('layer', ('groups', 'ex')), may hold values from -64 to 64
- query_grads: float32 [2, 1, 512, 1024], P('layer', 'pb', ('groups', 'ex')), may hold values from -64 to 64
- damping: float32 [2], P('layer'), may hold values from 0.05 to 0.5
Outputs:
- influence: float32 [1536, 1, 512], P(('groups', 'ex'), 'pb', 'layer')
All inputs are finite; a program needn't handle non-finite values.
Results may differ from a plain program's by a relative error of at most 0.0003.
Values sent between devices are 32-bit elements; how exact they have to be, the bound alone decides.
A program may use at most 64 MiB of HBM per device.

v0:
```python
import jax
import jax.numpy as jnp
from jax import lax
from jax.sharding import PartitionSpec as P


def solve_rows(factor, rows_in):
    inner = lax.linalg.triangular_solve(
        factor, rows_in, left_side=False, lower=True, transpose_a=True
    )
    return lax.linalg.triangular_solve(
        factor, inner, left_side=False, lower=True, transpose_a=False
    )


def on_device(train_grads, query_grads, damping):
    layers_here, local_rows, coords = train_grads.shape
    total_rows = local_rows * lax.axis_size("ex")
    half_rows = local_rows // lax.axis_size("pb")
    own_rows = lax.dynamic_slice_in_dim(train_grads, lax.axis_index("pb") * half_rows, half_rows, 1)
    partial_gram = jnp.einsum("lnp,lnq->lpq", own_rows, own_rows, precision=lax.Precision.HIGHEST)
    gram_matrix = lax.psum(partial_gram, ("ex", "pb"))
    identity = jnp.eye(coords, dtype=jnp.float32)
    fisher = gram_matrix / total_rows + damping[:, None, None] * identity[None]
    factor = jnp.linalg.cholesky(fisher)
    queries = query_grads[:, 0]
    solved = solve_rows(factor, queries)
    score_tile = jnp.einsum(
        "lnp,lkp->nk",
        train_grads,
        lax.all_gather(solved, "ex", axis=1, tiled=True),
        precision=lax.Precision.HIGHEST,
    )
    shares = lax.psum_scatter(score_tile, "layer", scatter_dimension=1, tiled=True)
    return shares[:, None, :]


def solution(mesh):
    in_specs = (
        P("layer", ("groups", "ex"), None),
        P("layer", "pb", ("groups", "ex"), None),
        P("layer"),
    )
    out_specs = P(("groups", "ex"), "pb", "layer")
    return jax.shard_map(
        on_device, mesh=mesh, in_specs=in_specs, out_specs=out_specs, check_vma=False
    )
```

profile of v0, /device:TPU:0, one launch (start us, length us, event | category | flops | bytes accessed | tf_op | source)
XLA Modules:
  0.0 545.7 jit_solution(9678609055191033883)
XLA Ops:
  7.5 5.0 convolution_bitcast_fusion
  13.3 113.3 %all-reduce.3.cloned.1.call-done = f32[1,1024,1024]{1,2,0:T(8,128)} async-done(((f32[1,1024,1024]{1,2,0:T(8,128)}), f32[1,1024,1024]{1,2,0:T(8,128)}) %all-reduce.3.cloned.1.call-update) | async-done | bytes 4194320 | tf_op jit(solution)/shard_map/psum | solution.py:22
  126.6 5.1 select_add_fusion
  131.7 5.6 %copy.5 = f32[1,1024,1024]{2,1,0:T(8,128)} copy(f32[1,1024,1024]{1,2,0:T(8,128)} %select_add_fusion) | data formatting | bytes 8388608 | tf_op jit(solution)/shard_map/add | solution.py:24
  143.7 11.7 %custom-call.72 = f32[1,128,128]{2,1,0:T(8,128)S(1)} custom-call(f32[1,128,128]{2,1,0:T(8,128)S(1)} %cholesky.582), custom_call_target="Cholesky" | custom-call | tf_op jit(solution)/shard_map/jit(cholesky)/cholesky | solution.py:25
  155.6 9.8 %custom-call.73 = f32[1,1,128,128]{2,3,1,0:T(8,128)S(1)} custom-call(f32[1,1,128,128]{3,2,1,0:T(8,128)S(1)} %get-tuple-element.40), custom_call_target="InvertDiagBlocksLowerTriangular" | custom-call | tf_op jit(solution)/shard_map/jit(cholesky)/cholesky | solution.py:25
  168.7 11.7 %custom-call.74 = f32[1,128,128]{2,1,0:T(8,128)S(1)} custom-call(f32[1,128,128]{2,1,0:T(8,128)S(1)} %cholesky.586), custom_call_target="Cholesky" | custom-call | tf_op jit(solution)/shard_map/jit(cholesky)/cholesky | solution.py:25
  184.4 9.8 %custom-call.75 = f32[1,1,128,128]{2,3,1,0:T(8,128)S(1)} custom-call(f32[1,1,128,128]{3,2,1,0:T(8,128)S(1)} %get-tuple-element.38), custom_call_target="InvertDiagBlocksLowerTriangular" | custom-call | tf_op jit(solution)/shard_map/jit(cholesky)/cholesky | solution.py:25
  198.9 11.7 %custom-call.76 = f32[1,128,128]{2,1,0:T(8,128)S(1)} custom-call(f32[1,128,128]{2,1,0:T(8,128)S(1)} %cholesky.591), custom_call_target="Cholesky" | custom-call | tf_op jit(solution)/shard_map/jit(cholesky)/cholesky | solution.py:25
  211.3 9.8 %custom-call.77 = f32[1,1,128,128]{2,3,1,0:T(8,128)S(1)} custom-call(f32[1,1,128,128]{3,2,1,0:T(8,128)S(1)} %get-tuple-element.36), custom_call_target="InvertDiagBlocksLowerTriangular" | custom-call | tf_op jit(solution)/shard_map/jit(cholesky)/cholesky | solution.py:25
  225.7 11.7 %custom-call.78 = f32[1,128,128]{2,1,0:T(8,128)S(1)} custom-call(f32[1,128,128]{2,1,0:T(8,128)S(1)} %cholesky.596), custom_call_target="Cholesky" | custom-call | tf_op jit(solution)/shard_map/jit(cholesky)/cholesky | solution.py:25
  238.2 9.8 %custom-call.79 = f32[1,1,128,128]{2,3,1,0:T(8,128)S(1)} custom-call(f32[1,1,128,128]{3,2,1,0:T(8,128)S(1)} %get-tuple-element.34), custom_call_target="InvertDiagBlocksLowerTriangular" | custom-call | tf_op jit(solution)/shard_map/jit(cholesky)/cholesky | solution.py:25
  252.3 11.9 %custom-call.80 = f32[1,128,128]{2,1,0:T(8,128)S(1)} custom-call(f32[1,128,128]{2,1,0:T(8,128)S(1)} %cholesky.601), custom_call_target="Cholesky" | custom-call | tf_op jit(solution)/shard_map/jit(cholesky)/cholesky | solution.py:25
  265.0 9.8 %custom-call.81 = f32[1,1,128,128]{2,3,1,0:T(8,128)S(1)} custom-call(f32[1,1,128,128]{3,2,1,0:T(8,128)S(1)} %get-tuple-element.32), custom_call_target="InvertDiagBlocksLowerTriangular" | custom-call | tf_op jit(solution)/shard_map/jit(cholesky)/cholesky | solution.py:25
  279.0 11.7 %custom-call.82 = f32[1,128,128]{2,1,0:T(8,128)S(1)} custom-call(f32[1,128,128]{2,1,0:T(8,128)S(1)} %cholesky.606), custom_call_target="Cholesky" | custom-call | tf_op jit(solution)/shard_map/jit(cholesky)/cholesky | solution.py:25
  291.5 9.8 %custom-call.83 = f32[1,1,128,128]{2,3,1,0:T(8,128)S(1)} custom-call(f32[1,1,128,128]{3,2,1,0:T(8,128)S(1)} %get-tuple-element.30), custom_call_target="InvertDiagBlocksLowerTriangular" | custom-call | tf_op jit(solution)/shard_map/jit(cholesky)/cholesky | solution.py:25
  305.4 11.7 %custom-call.84 = f32[1,128,128]{2,1,0:T(8,128)S(1)} custom-call(f32[1,128,128]{2,1,0:T(8,128)S(1)} %cholesky.611), custom_call_target="Cholesky" | custom-call | tf_op jit(solution)/shard_map/jit(cholesky)/cholesky | solution.py:25
  317.9 9.8 %custom-call.85 = f32[1,1,128,128]{2,3,1,0:T(8,128)S(1)} custom-call(f32[1,1,128,128]{3,2,1,0:T(8,128)S(1)} %get-tuple-element.28), custom_call_target="InvertDiagBlocksLowerTriangular" | custom-call | tf_op jit(solution)/shard_map/jit(cholesky)/cholesky | solution.py:25
  330.7 11.7 %custom-call.86 = f32[1,128,128]{2,1,0:T(8,128)S(1)} custom-call(f32[1,128,128]{2,1,0:T(8,128)S(1)} %fusion.18), custom_call_target="Cholesky" | custom-call | tf_op jit(solution)/shard_map/jit(cholesky)/cholesky | solution.py:25
  352.9 4.9 select_select_fusion
  357.8 23.7 %while.1 = (s32[]{:T(128)}, f32[1,1024,1024]{1,2,0:T(8,128)}, s32[8,2]{0,1:T(2,128)S(1)}, f32[8,1,128,128]{3,2,1,0:T(8,128)S(1)}, s32[]{:T(128)}) while((s32[]{:T(128)}, f32[1,1024,1024]{1,2,0:T(8,128)}, s32[8,2]{0,1:T(2,128)S(1)}, f32[8,1,128,128]{3,2,1,0:T(8,128)S(1)}, s32[]{:T(128)}) %tuple.49), condition=%wide.while_cond, body=%wide.while_body.sunk | while | flops 2 | bytes 393333 | solution.py:8
  381.5 78.8 %custom-call.87 = f32[1,8,128,128]{2,3,1,0:T(8,128)S(1)} custom-call(f32[1,8,128,128]{3,2,1,0:T(8,128)S(1)} %bitcast.460), custom_call_target="InvertDiagBlocksLowerTriangular" | custom-call | tf_op jit(solution)/shard_map/triangular_solve | solution.py:8
  482.3 40.7 %all-gather.2.cloned.1.call-done = f32[1,512,1024]{2,1,0:T(8,128)} async-done(((f32[1,32,1024]{2,1,0:T(8,128)}), f32[1,512,1024]{2,1,0:T(8,128)}) %all-gather.2.cloned.1.call-update) | async-done | bytes 2097168 | tf_op jit(solution)/shard_map/all_gather | solution.py:31
  527.5 9.9 %reduce-scatter.2.cloned.1.call-done = f32[96,256]{1,0:T(8,128)} async-done(((f32[96,512]{1,0:T(8,128)}), f32[96,256]{1,0:T(8,128)}) %reduce-scatter.2.cloned.1.call-update) | async-done | bytes 98320 | tf_op jit(solution)/shard_map/reduce_scatter | solution.py:34
  (166 shorter events, 100.1 us)
Async XLA Ops:
  6.5 1.0 copy-start
  6.5 120.0 %all-reduce.3.cloned.1.call-start = ((), (), s32[]{:S(2)}) async-start(), calls=%async_computation.1 | async-start | bytes 8388608 | tf_op jit(solution)/shard_map/psum | solution.py:22
  12.6 510.4 %all-gather.2.cloned.1.call-start = ((), (), s32[]{:S(2)}) async-start(), calls=%async_computation.2 | async-start | bytes 2228224 | tf_op jit(solution)/shard_map/all_gather | solution.py:31
  141.8 1.9 copy-start.1
  352.9 107.4 %copy-start.3 = (f32[1,1,32,1024]{3,2,1,0:T(8,128)S(1)}, f32[1,1,32,1024]{3,2,1,0:T(8,128)}, u32[]{:S(2)}) copy-start(f32[1,1,32,1024]{3,2,1,0:T(8,128)} %param.4) | copy-start | bytes 393220
  481.6 0.7 copy-start.2
  482.3 55.1 %reduce-scatter.2.cloned.1.call-start = ((), (), s32[]{:S(2)}) async-start(), calls=%async_computation.3 | async-start | bytes 294912 | tf_op jit(solution)/shard_map/reduce_scatter | solution.py:34
Sparse Core Ops, SparseCore 0:
  12.7 113.8 all-reduce.2
  482.4 40.5 all-gather.1
  527.6 9.7 reduce-scatter.1
where the time goes:
time: 550 us; the launch traced here: 546 us
  other arithmetic  261 us (47%)
  waiting for transfers between devices  164 us (30%)
  matrix products  57.3 us (10%)
  local copies, waits for them, and re-layouts  43.8 us (8%)
  between operations  19.7 us (4%)
    another operation x30, other arithmetic, on_device(): factor = jnp.linalg.cholesky(fisher)  168 us
    psum x1, waiting for transfers between devices, on_device(): gram_matrix = lax.psum(partial_gram, ('ex', 'pb'))  113 us
    another operation x3, other arithmetic, solve_rows(): lax.linalg.triangular_solve(factor, rows_in, left_side=False, lower=True,...  83.6 us
    all_gather x1, waiting for transfers between devices, on_device(): lax.all_gather(solved, 'ex', axis=1, tiled=True)  40.7 us
    another operation x14, matrix products, on_device(): factor = jnp.linalg.cholesky(fisher)  27.2 us
    another operation x40, local copies, waits for them, and re-layouts  23.5 us
  transfers between devices with their start and end apart: 3, of which 3 were waited for; matrix products, arithmetic and copies ran while one was open for 0% of the time, Pallas kernels for 0%

commit v1 on v0

--- a/solution.py
+++ b/solution.py
@@ -25,12 +25,21 @@
     factor = jnp.linalg.cholesky(fisher)
     queries = query_grads[:, 0]
     solved = solve_rows(factor, queries)
-    score_tile = jnp.einsum(
-        "lnp,lkp->nk",
-        train_grads,
-        lax.all_gather(solved, "ex", axis=1, tiled=True),
-        precision=lax.Precision.HIGHEST,
-    )
+    ways, here, hop = (lax.axis_size("ex"), lax.axis_index("ex"), solved.shape[1])
+    earlier, later = ([], [])
+    going_up = going_down = solved
+    for far in range(ways // 2 + 1):
+        earlier.append(
+            jnp.einsum("lnp,lkp->nk", train_grads, going_up, precision=lax.Precision.HIGHEST)
+        )
+        if 0 < far < ways - ways // 2:
+            later.append(
+                jnp.einsum("lnp,lkp->nk", train_grads, going_down, precision=lax.Precision.HIGHEST)
+            )
+        going_up = lax.ppermute(going_up, "ex", [(d, (d + 1) % ways) for d in range(ways)])
+        going_down = lax.ppermute(going_down, "ex", [(d, (d - 1) % ways) for d in range(ways)])
+    line = jnp.concatenate([*earlier[::-1], *later], axis=1)
+    score_tile = jnp.roll(line, (here - ways // 2) * earlier[0].shape[1], axis=1)
     shares = lax.psum_scatter(score_tile, "layer", scatter_dimension=1, tiled=True)
     return shares[:, None, :]
 

time: 550 us -> 570 us (1.036)
  starting transfers between devices: 0.09 us -> 31.4 us
  waiting for transfers between devices: 164 us -> 148 us
    all_gather x1 -> x0, waiting for transfers between devices: 40.7 us -> none  [on_device(): lax.all_gather(solved, 'ex', axis=1, tiled=True)]
    ppermute x0 -> x15, starting transfers between devices: none -> 31.4 us  [the longest x7 31.3 us: on_device(): lax.ppermute(going_down, 'ex', [(d, (d - 1) % ways) for d in range(ways)])]
    ppermute x0 -> x15, waiting for transfers between devices: none -> 26 us  [the longest x8 26 us: on_device(): lax.ppermute(going_up, 'ex', [(d, (d + 1) % ways) for d in range(ways)])]
  transfers between devices with their start and end apart: 3 -> 17, of which waited for: 3 -> 10; matrix products, arithmetic and copies ran while one was open for 0% -> 1% of each run, Pallas kernels for 0% -> 0%
where the time goes in v1:
time: 570 us; the launch traced here: 566 us
  other arithmetic  261 us (46%)
  waiting for transfers between devices  148 us (26%)
  matrix products  60.8 us (11%)
  local copies, waits for them, and re-layouts  43.9 us (8%)
  starting transfers between devices  31.4 us (6%)
  between operations  20.3 us (4%)
    another operation x30, other arithmetic, on_device(): factor = jnp.linalg.cholesky(fisher)  168 us
    psum x1, waiting for transfers between devices, on_device(): gram_matrix = lax.psum(partial_gram, ('ex', 'pb'))  113 us
    another operation x3, other arithmetic, solve_rows(): lax.linalg.triangular_solve(factor, rows_in, left_side=False, lower=True,...  83.7 us
    ppermute x7, starting transfers between devices, on_device(): lax.ppermute(going_down, 'ex', [(d, (d - 1) % ways) for d in range(ways)])  31.3 us
    another operation x14, matrix products, on_device(): factor = jnp.linalg.cholesky(fisher)  26.9 us
    ppermute x8, waiting for transfers between devices, on_device(): lax.ppermute(going_up, 'ex', [(d, (d + 1) % ways) for d in range(ways)])  26 us
    another operation x40, local copies, waits for them, and re-layouts  23.5 us
  transfers between devices with their start and end apart: 17, of which 10 were waited for; matrix products, arithmetic and copies ran while one was open for 1% of the time, Pallas kernels for 0%

profile of v1, /device:TPU:0, one launch (start us, length us, event | category | flops | bytes accessed | tf_op | source)
XLA Modules:
  0.0 566.2 jit_solution(15708218522211460485)
XLA Ops:
  7.5 5.0 convolution_bitcast_fusion
  13.3 113.3 %all-reduce.3.cloned.1.call-done = f32[1,1024,1024]{1,2,0:T(8,128)} async-done(((f32[1,1024,1024]{1,2,0:T(8,128)}), f32[1,1024,1024]{1,2,0:T(8,128)}) %all-reduce.3.cloned.1.call-update) | async-done | bytes 4194320 | tf_op jit(solution)/shard_map/psum | solution.py:22
  126.6 5.1 select_add_fusion
  131.7 5.9 %copy.5 = f32[1,1024,1024]{2,1,0:T(8,128)} copy(f32[1,1024,1024]{1,2,0:T(8,128)} %select_add_fusion) | data formatting | bytes 8388608 | tf_op jit(solution)/shard_map/add | solution.py:24
  144.0 11.7 %custom-call.72 = f32[1,128,128]{2,1,0:T(8,128)S(1)} custom-call(f32[1,128,128]{2,1,0:T(8,128)S(1)} %cholesky.582), custom_call_target="Cholesky" | custom-call | tf_op jit(solution)/shard_map/jit(cholesky)/cholesky | solution.py:25
  155.9 9.8 %custom-call.73 = f32[1,1,128,128]{2,3,1,0:T(8,128)S(1)} custom-call(f32[1,1,128,128]{3,2,1,0:T(8,128)S(1)} %get-tuple-element.40), custom_call_target="InvertDiagBlocksLowerTriangular" | custom-call | tf_op jit(solution)/shard_map/jit(cholesky)/cholesky | solution.py:25
  169.0 11.7 %custom-call.74 = f32[1,128,128]{2,1,0:T(8,128)S(1)} custom-call(f32[1,128,128]{2,1,0:T(8,128)S(1)} %cholesky.586), custom_call_target="Cholesky" | custom-call | tf_op jit(solution)/shard_map/jit(cholesky)/cholesky | solution.py:25
  184.3 9.8 %custom-call.75 = f32[1,1,128,128]{2,3,1,0:T(8,128)S(1)} custom-call(f32[1,1,128,128]{3,2,1,0:T(8,128)S(1)} %get-tuple-element.38), custom_call_target="InvertDiagBlocksLowerTriangular" | custom-call | tf_op jit(solution)/shard_map/jit(cholesky)/cholesky | solution.py:25
  198.8 11.7 %custom-call.76 = f32[1,128,128]{2,1,0:T(8,128)S(1)} custom-call(f32[1,128,128]{2,1,0:T(8,128)S(1)} %cholesky.591), custom_call_target="Cholesky" | custom-call | tf_op jit(solution)/shard_map/jit(cholesky)/cholesky | solution.py:25
  211.3 9.8 %custom-call.77 = f32[1,1,128,128]{2,3,1,0:T(8,128)S(1)} custom-call(f32[1,1,128,128]{3,2,1,0:T(8,128)S(1)} %get-tuple-element.36), custom_call_target="InvertDiagBlocksLowerTriangular" | custom-call | tf_op jit(solution)/shard_map/jit(cholesky)/cholesky | solution.py:25
  225.7 11.7 %custom-call.78 = f32[1,128,128]{2,1,0:T(8,128)S(1)} custom-call(f32[1,128,128]{2,1,0:T(8,128)S(1)} %cholesky.596), custom_call_target="Cholesky" | custom-call | tf_op jit(solution)/shard_map/jit(cholesky)/cholesky | solution.py:25
  238.2 9.8 %custom-call.79 = f32[1,1,128,128]{2,3,1,0:T(8,128)S(1)} custom-call(f32[1,1,128,128]{3,2,1,0:T(8,128)S(1)} %get-tuple-element.34), custom_call_target="InvertDiagBlocksLowerTriangular" | custom-call | tf_op jit(solution)/shard_map/jit(cholesky)/cholesky | solution.py:25
  252.3 12.1 %custom-call.80 = f32[1,128,128]{2,1,0:T(8,128)S(1)} custom-call(f32[1,128,128]{2,1,0:T(8,128)S(1)} %cholesky.601), custom_call_target="Cholesky" | custom-call | tf_op jit(solution)/shard_map/jit(cholesky)/cholesky | solution.py:25
  265.1 9.8 %custom-call.81 = f32[1,1,128,128]{2,3,1,0:T(8,128)S(1)} custom-call(f32[1,1,128,128]{3,2,1,0:T(8,128)S(1)} %get-tuple-element.32), custom_call_target="InvertDiagBlocksLowerTriangular" | custom-call | tf_op jit(solution)/shard_map/jit(cholesky)/cholesky | solution.py:25
  279.2 11.7 %custom-call.82 = f32[1,128,128]{2,1,0:T(8,128)S(1)} custom-call(f32[1,128,128]{2,1,0:T(8,128)S(1)} %cholesky.606), custom_call_target="Cholesky" | custom-call | tf_op jit(solution)/shard_map/jit(cholesky)/cholesky | solution.py:25
  291.7 9.8 %custom-call.83 = f32[1,1,128,128]{2,3,1,0:T(8,128)S(1)} custom-call(f32[1,1,128,128]{3,2,1,0:T(8,128)S(1)} %get-tuple-element.30), custom_call_target="InvertDiagBlocksLowerTriangular" | custom-call | tf_op jit(solution)/shard_map/jit(cholesky)/cholesky | solution.py:25
  305.3 11.7 %custom-call.84 = f32[1,128,128]{2,1,0:T(8,128)S(1)} custom-call(f32[1,128,128]{2,1,0:T(8,128)S(1)} %cholesky.611), custom_call_target="Cholesky" | custom-call | tf_op jit(solution)/shard_map/jit(cholesky)/cholesky | solution.py:25
  317.8 9.8 %custom-call.85 = f32[1,1,128,128]{2,3,1,0:T(8,128)S(1)} custom-call(f32[1,1,128,128]{3,2,1,0:T(8,128)S(1)} %get-tuple-element.28), custom_call_target="InvertDiagBlocksLowerTriangular" | custom-call | tf_op jit(solution)/shard_map/jit(cholesky)/cholesky | solution.py:25
  330.6 11.7 %custom-call.86 = f32[1,128,128]{2,1,0:T(8,128)S(1)} custom-call(f32[1,128,128]{2,1,0:T(8,128)S(1)} %fusion.13), custom_call_target="Cholesky" | custom-call | tf_op jit(solution)/shard_map/jit(cholesky)/cholesky | solution.py:25
  352.9 4.9 select_select_fusion
  357.8 23.7 %while.1 = (s32[]{:T(128)}, f32[1,1024,1024]{1,2,0:T(8,128)}, s32[8,2]{0,1:T(2,128)S(1)}, f32[8,1,128,128]{3,2,1,0:T(8,128)S(1)}, s32[]{:T(128)}) while((s32[]{:T(128)}, f32[1,1024,1024]{1,2,0:T(8,128)}, s32[8,2]{0,1:T(2,128)S(1)}, f32[8,1,128,128]{3,2,1,0:T(8,128)S(1)}, s32[]{:T(128)}) %tuple.65), condition=%wide.while_cond, body=%wide.while_body.sunk | while | flops 2 | bytes 393333 | solution.py:8
  381.5 78.8 %custom-call.87 = f32[1,8,128,128]{2,3,1,0:T(8,128)S(1)} custom-call(f32[1,8,128,128]{3,2,1,0:T(8,128)S(1)} %bitcast.627), custom_call_target="InvertDiagBlocksLowerTriangular" | custom-call | tf_op jit(solution)/shard_map/triangular_solve | solution.py:8
  481.7 7.1 %collective-permute-done = f32[1,32,1024]{2,1,0:T(8,128)S(1)} collective-permute-done((f32[1,32,1024]{2,1,0:T(8,128)S(1)}, f32[1,32,1024]{2,1,0:T(8,128)S(1)}, u32[]{:S(2)}, u32[]{:S(2)}) %collective-permute-start) | collective-permute-done | bytes 131104 | tf_op jit(solution)/shard_map/ppermute | solution.py:39
  548.3 9.1 %reduce-scatter.2.cloned.1.call-done = f32[96,256]{0,1:T(8,128)} async-done(((f32[96,512]{0,1:T(8,128)}), f32[96,256]{0,1:T(8,128)}) %reduce-scatter.2.cloned.1.call-update) | async-done | bytes 98320 | tf_op jit(solution)/shard_map/reduce_scatter | solution.py:43
  (223 shorter events, 153.7 us)
Async XLA Ops:
  6.5 1.0 copy-start
  6.5 120.1 %all-reduce.3.cloned.1.call-start = ((), (), s32[]{:S(2)}) async-start(), calls=%async_computation.1 | async-start | bytes 8388608 | tf_op jit(solution)/shard_map/psum | solution.py:22
  12.6 544.9 %reduce-scatter.2.cloned.1.call-start = ((), (), s32[]{:S(2)}) async-start(), calls=%async_computation.2 | async-start | bytes 393216 | tf_op jit(solution)/shard_map/reduce_scatter | solution.py:43
  142.1 1.9 copy-start.1
  352.9 107.4 %copy-start.2 = (f32[1,1,32,1024]{3,2,1,0:T(8,128)S(1)}, f32[1,1,32,1024]{3,2,1,0:T(8,128)}, u32[]{:S(2)}) copy-start(f32[1,1,32,1024]{3,2,1,0:T(8,128)} %param.4) | copy-start | bytes 393220
  481.6 7.1 %collective-permute-start = (f32[1,32,1024]{2,1,0:T(8,128)S(1)}, f32[1,32,1024]{2,1,0:T(8,128)S(1)}, u32[]{:S(2)}, u32[]{:S(2)}) collective-permute-start(f32[1,32,1024]{2,1,0:T(8,128)S(1)} %constant_dynamic-update-slice_fusion.36), channel_id=1, source_target_pairs={{0,2},{2,4},{4,6},{6,8},{8,10},{10,12},{12,14},{14,16},{16,18},{18... | collective-permute-start | bytes 393224 | tf_op jit(solution)/shard_map/ppermute | solution.py:39
  488.8 7.2 %collective-permute-start.1 = (f32[1,32,1024]{2,1,0:T(8,128)S(1)}, f32[1,32,1024]{2,1,0:T(8,128)S(1)}, u32[]{:S(2)}, u32[]{:S(2)}) collective-permute-start(f32[1,32,1024]{2,1,0:T(8,128)S(1)} %collective-permute-done), channel_id=1, source_target_pairs={{0,2},{2,4},{4,6},{6,8},{8,10},{10,12},{12,14},{14,16},{16,18},{18... | collective-permute-start | bytes 393224 | tf_op jit(solution)/shard_map/ppermute | solution.py:39
  488.8 7.2 %collective-permute-start.8 = (f32[1,32,1024]{2,1,0:T(8,128)S(1)}, f32[1,32,1024]{2,1,0:T(8,128)S(1)}, u32[]{:S(2)}, u32[]{:S(2)}) collective-permute-start(f32[1,32,1024]{2,1,0:T(8,128)S(1)} %constant_dynamic-update-slice_fusion.36), channel_id=1, source_target_pairs={{0,30},{2,0},{4,2},{6,4},{8,6},{10,8},{12,10},{14,12},{16,14},{18,... | collective-permute-start | bytes 393224 | tf_op jit(solution)/shard_map/ppermute | solution.py:40
  496.0 7.2 %collective-permute-start.2 = (f32[1,32,1024]{2,1,0:T(8,128)S(1)}, f32[1,32,1024]{2,1,0:T(8,128)S(1)}, u32[]{:S(2)}, u32[]{:S(2)}) collective-permute-start(f32[1,32,1024]{2,1,0:T(8,128)S(1)} %collective-permute-done.1), channel_id=1, source_target_pairs={{0,2},{2,4},{4,6},{6,8},{8,10},{10,12},{12,14},{14,16},{16,18},{18... | collective-permute-start | bytes 393224 | tf_op jit(solution)/shard_map/ppermute | solution.py:39
  496.0 7.2 %collective-permute-start.9 = (f32[1,32,1024]{2,1,0:T(8,128)S(1)}, f32[1,32,1024]{2,1,0:T(8,128)S(1)}, u32[]{:S(2)}, u32[]{:S(2)}) collective-permute-start(f32[1,32,1024]{2,1,0:T(8,128)S(1)} %collective-permute-done.8), channel_id=1, source_target_pairs={{0,30},{2,0},{4,2},{6,4},{8,6},{10,8},{12,10},{14,12},{16,14},{18,... | collective-permute-start | bytes 393224 | tf_op jit(solution)/shard_map/ppermute | solution.py:40
  503.2 7.2 %collective-permute-start.3 = (f32[1,32,1024]{2,1,0:T(8,128)S(1)}, f32[1,32,1024]{2,1,0:T(8,128)S(1)}, u32[]{:S(2)}, u32[]{:S(2)}) collective-permute-start(f32[1,32,1024]{2,1,0:T(8,128)S(1)} %collective-permute-done.2), channel_id=1, source_target_pairs={{0,2},{2,4},{4,6},{6,8},{8,10},{10,12},{12,14},{14,16},{16,18},{18... | collective-permute-start | bytes 393224 | tf_op jit(solution)/shard_map/ppermute | solution.py:39
  503.2 7.2 %collective-permute-start.10 = (f32[1,32,1024]{2,1,0:T(8,128)S(1)}, f32[1,32,1024]{2,1,0:T(8,128)S(1)}, u32[]{:S(2)}, u32[]{:S(2)}) collective-permute-start(f32[1,32,1024]{2,1,0:T(8,128)S(1)} %collective-permute-done.9), channel_id=1, source_target_pairs={{0,30},{2,0},{4,2},{6,4},{8,6},{10,8},{12,10},{14,12},{16,14},{18,... | collective-permute-start | bytes 393224 | tf_op jit(solution)/shard_map/ppermute | solution.py:40
  510.4 7.2 %collective-permute-start.4 = (f32[1,32,1024]{2,1,0:T(8,128)S(1)}, f32[1,32,1024]{2,1,0:T(8,128)S(1)}, u32[]{:S(2)}, u32[]{:S(2)}) collective-permute-start(f32[1,32,1024]{2,1,0:T(8,128)S(1)} %collective-permute-done.3), channel_id=1, source_target_pairs={{0,2},{2,4},{4,6},{6,8},{8,10},{10,12},{12,14},{14,16},{16,18},{18... | collective-permute-start | bytes 393224 | tf_op jit(solution)/shard_map/ppermute | solution.py:39
  510.4 7.2 %collective-permute-start.11 = (f32[1,32,1024]{2,1,0:T(8,128)S(1)}, f32[1,32,1024]{2,1,0:T(8,128)S(1)}, u32[]{:S(2)}, u32[]{:S(2)}) collective-permute-start(f32[1,32,1024]{2,1,0:T(8,128)S(1)} %collective-permute-done.10), channel_id=1, source_target_pairs={{0,30},{2,0},{4,2},{6,4},{8,6},{10,8},{12,10},{14,12},{16,14},{18,... | collective-permute-start | bytes 393224 | tf_op jit(solution)/shard_map/ppermute | solution.py:40
  517.5 7.2 %collective-permute-start.5 = (f32[1,32,1024]{2,1,0:T(8,128)S(1)}, f32[1,32,1024]{2,1,0:T(8,128)S(1)}, u32[]{:S(2)}, u32[]{:S(2)}) collective-permute-start(f32[1,32,1024]{2,1,0:T(8,128)S(1)} %collective-permute-done.4), channel_id=1, source_target_pairs={{0,2},{2,4},{4,6},{6,8},{8,10},{10,12},{12,14},{14,16},{16,18},{18... | collective-permute-start | bytes 393224 | tf_op jit(solution)/shard_map/ppermute | solution.py:39
  517.5 7.2 %collective-permute-start.12 = (f32[1,32,1024]{2,1,0:T(8,128)S(1)}, f32[1,32,1024]{2,1,0:T(8,128)S(1)}, u32[]{:S(2)}, u32[]{:S(2)}) collective-permute-start(f32[1,32,1024]{2,1,0:T(8,128)S(1)} %collective-permute-done.11), channel_id=1, source_target_pairs={{0,30},{2,0},{4,2},{6,4},{8,6},{10,8},{12,10},{14,12},{16,14},{18,... | collective-permute-start | bytes 393224 | tf_op jit(solution)/shard_map/ppermute | solution.py:40
  524.7 7.2 %collective-permute-start.6 = (f32[1,32,1024]{2,1,0:T(8,128)S(1)}, f32[1,32,1024]{2,1,0:T(8,128)S(1)}, u32[]{:S(2)}, u32[]{:S(2)}) collective-permute-start(f32[1,32,1024]{2,1,0:T(8,128)S(1)} %collective-permute-done.5), channel_id=1, source_target_pairs={{0,2},{2,4},{4,6},{6,8},{8,10},{10,12},{12,14},{14,16},{16,18},{18... | collective-permute-start | bytes 393224 | tf_op jit(solution)/shard_map/ppermute | solution.py:39
  524.7 7.2 %collective-permute-start.13 = (f32[1,32,1024]{2,1,0:T(8,128)S(1)}, f32[1,32,1024]{2,1,0:T(8,128)S(1)}, u32[]{:S(2)}, u32[]{:S(2)}) collective-permute-start(f32[1,32,1024]{2,1,0:T(8,128)S(1)} %collective-permute-done.12), channel_id=1, source_target_pairs={{0,30},{2,0},{4,2},{6,4},{8,6},{10,8},{12,10},{14,12},{16,14},{18,... | collective-permute-start | bytes 393224 | tf_op jit(solution)/shard_map/ppermute | solution.py:40
  531.9 7.1 %collective-permute-start.7 = (f32[1,32,1024]{2,1,0:T(8,128)S(1)}, f32[1,32,1024]{2,1,0:T(8,128)S(1)}, u32[]{:S(2)}, u32[]{:S(2)}) collective-permute-start(f32[1,32,1024]{2,1,0:T(8,128)S(1)} %collective-permute-done.6), channel_id=1, source_target_pairs={{0,2},{2,4},{4,6},{6,8},{8,10},{10,12},{12,14},{14,16},{16,18},{18... | collective-permute-start | bytes 393224 | tf_op jit(solution)/shard_map/ppermute | solution.py:39
  531.9 14.9 %collective-permute-start.14 = (f32[1,32,1024]{2,1,0:T(8,128)S(1)}, f32[1,32,1024]{2,1,0:T(8,128)S(1)}, u32[]{:S(2)}, u32[]{:S(2)}) collective-permute-start(f32[1,32,1024]{2,1,0:T(8,128)S(1)} %collective-permute-done.13), channel_id=1, source_target_pairs={{0,30},{2,0},{4,2},{6,4},{8,6},{10,8},{12,10},{14,12},{16,14},{18,... | collective-permute-start | bytes 393224 | tf_op jit(solution)/shard_map/ppermute | solution.py:40
Sparse Core Ops, SparseCore 0:
  12.7 113.8 all-reduce.2
  548.4 8.9 reduce-scatter.1
